TPU v7x, 32 devices: a whole 2x2x4 slice. The times are simulated.
32 devices in a mesh: grp: 2 (over x), gx: 8 (over z, y), gy: 2 (over core).
Axes of the slice: x: 2, y: 2, z: 4, core: 2. Of those that a mesh axis runs over, the one named last changes fastest.
Arguments:
- spectrum: float32 [16, 96, 1152], P('gx', 'gy', 'grp'), may hold values from 0 to 2
- wet_mask: int32 [16, 96], P('gx', 'gy'), may hold values 0 or 1
- ocean_source: int32 [16, 96], P('gx', 'gy'), may hold values from 0 to 95
- ocean_u: float32 [16, 96, 40], P('gx', 'gy', 'grp'), may hold values from -2 to 2
- ocean_v: float32 [16, 96, 40], P('gx', 'gy', 'grp'), may hold values from -2 to 2
- current_weights: float32 [40, 32], replicated, may hold values from 0.005 to 0.04
- drift_weights: float32 [40, 32], replicated, may hold values from 0.005 to 0.05
- inter_left: bfloat16 [1152, 512], P('grp'), may hold values from -0.25 to 0.25
- inter_right: bfloat16 [1152, 512], P('grp'), may hold values from -0.25 to 0.25
- inter_out: bfloat16 [512, 1152], P(None, 'grp'), may hold values from -0.25 to 0.25
- mixing: float32 [40, 40], P(None, 'grp'), may hold values from -0.47434166 to 0.47434166
Outputs:
- spectrum_out: float32 [16, 96, 1152], P('gx', 'gy', 'grp')
- ocean_u_out: float32 [16, 96, 40], P('gx', 'gy', 'grp')
- ocean_v_out: float32 [16, 96, 40], P('gx', 'gy', 'grp')
- drift_u: float32 [16, 96, 40], P('gx', 'gy', 'grp')
- drift_v: float32 [16, 96, 40], P('gx', 'gy', 'grp')
Inputs may be any that keep to these rules, and one draw needn't show every extreme that they name: `wet_mask`: 1 marks a sea column, 0 a land column. `ocean_source`: each entry numbers a column of the same tile of 2 x 48 columns as (x mod 2) * 48 + (y mod 48).
All inputs are finite; a program needn't handle non-finite values. No bound on the sum of `wet_mask` on one device may be relied on, other than what follows from the above.
Results may differ from a plain program's by a relative error of at most 0.00077.
Values sent between devices are 32-bit elements; how exact they have to be, the bound alone decides.
A program may use at most 64 MiB of HBM per device.

v0:
```python
import jax
import jax.numpy as jnp
from jax import lax
from jax.sharding import PartitionSpec as P

NF = 32
ND = 36
NLEV = 40
WAVE_SECTIONS = 3
OCEAN_SECTIONS = 2
NFL = 16
highest = lax.Precision.HIGHEST
inter_step = 0.1
ocean_step = 0.4
coriolis = 0.5
viscosity = 0.1


def extended(array, sides, width):
    for axis, dim in sides:
        size, length = (lax.axis_size(axis), array.shape[dim])
        up = [(i, (i + 1) % size) for i in range(size - 1)]
        down = [(j, i) for i, j in up]
        last = lax.slice_in_dim(array, length - width, length, axis=dim)
        leading = lax.slice_in_dim(array, 0, width, axis=dim)
        before = lax.ppermute(last, axis, up)
        after = lax.ppermute(leading, axis, down)
        array = jnp.concatenate([before, array, after], axis=dim)
    return array


def bin_tables(band_index, bin_count):
    position = jnp.arange(bin_count)
    direction = (position // NFL).astype(jnp.float32)
    frequency = (band_index * NFL + position % NFL).astype(jnp.float32)
    angle_value = 2.0 * jnp.pi * direction / ND
    group_speed = 0.2 + 0.4 * (NF - 1 - frequency) / (NF - 1)
    turning = 0.5 * (frequency + 1.0) / NF
    return (jnp.cos(angle_value), jnp.sin(angle_value), group_speed, turning)


def beam_sweep(padded, velocity, which_axis):
    extent = velocity.shape[which_axis]

    def take_part(offset):
        return lax.slice_in_dim(padded, offset, offset + extent, axis=which_axis)

    centre = take_part(2)
    upwind_one = jnp.where(velocity >= 0.0, take_part(1), take_part(3))
    beyond = jnp.where(velocity >= 0.0, take_part(0), take_part(4))
    magnitude = jnp.abs(velocity)
    return (
        centre
        - 0.5 * magnitude * (3.0 * centre - 4.0 * upwind_one + beyond)
        + 0.5 * magnitude * magnitude * (centre - 2.0 * upwind_one + beyond)
    )


def body(
    spectrum,
    wet_mask,
    ocean_source,
    ocean_u,
    ocean_v,
    current_weights,
    drift_weights,
    inter_left,
    inter_right,
    inter_out,
    mixing,
):
    band_index = lax.axis_index("grp")
    tile_x = spectrum.shape[0]
    tile_y = spectrum.shape[1]
    bin_count = spectrum.shape[2]
    levels_own = ocean_u.shape[2]
    cosine, sine_value, group_speed, turning = bin_tables(band_index, bin_count)
    wet_factor = wet_mask.astype(jnp.float32)[:, :, None]
    flat_source = ocean_source.reshape(-1)
    whole_u, whole_v = (
        lax.all_gather(ocean_u, "grp", axis=2, tiled=True),
        lax.all_gather(ocean_v, "grp", axis=2, tiled=True),
    )
    weights_band = lax.dynamic_slice_in_dim(current_weights, band_index * NFL, NFL, 1)
    picked_u = jnp.take(whole_u.reshape(tile_x * tile_y, NLEV), flat_source, axis=0)
    picked_v = jnp.take(whole_v.reshape(tile_x * tile_y, NLEV), flat_source, axis=0)
    flow_x = jnp.dot(picked_u, weights_band, precision=highest, preferred_element_type=jnp.float32)
    flow_y = jnp.dot(picked_v, weights_band, precision=highest, preferred_element_type=jnp.float32)
    flow_x = flow_x.reshape(tile_x, tile_y, NFL)
    flow_y = flow_y.reshape(tile_x, tile_y, NFL)
    flow_x_bins = jnp.tile(flow_x, (1, 1, ND))
    flow_y_bins = jnp.tile(flow_y, (1, 1, ND))
    speed_y = group_speed * sine_value + flow_y_bins
    turn_rate = turning * (sine_value * flow_x_bins - cosine * flow_y_bins)
    current_pad = extended(jnp.concatenate([flow_x, flow_y], axis=2), (("gx", 0), ("gy", 1)), 2)
    speed_x_wide = group_speed * cosine + jnp.tile(current_pad[2 : tile_x + 2, :, :NFL], (1, 1, ND))
    spectrum_now = wet_factor * spectrum
    for repeat in range(WAVE_SECTIONS):
        padded = extended(spectrum_now, (("gx", 0), ("gy", 1)), 2)
        shifted = beam_sweep(padded, speed_x_wide, 0)
        shifted = beam_sweep(shifted, speed_y, 1)
        behind = jnp.roll(shifted, NFL, axis=2)
        ahead_dir = jnp.roll(shifted, -NFL, axis=2)
        upwind = jnp.where(turn_rate >= 0.0, behind, ahead_dir)
        turned = shifted - jnp.abs(turn_rate) * (shifted - upwind)
        flat_bins = spectrum_now.reshape(-1, bin_count).astype(jnp.bfloat16)
        product = jnp.dot(flat_bins, inter_left, preferred_element_type=jnp.float32) * jnp.dot(
            flat_bins, inter_right, preferred_element_type=jnp.float32
        )
        source = inter_step * jnp.dot(
            product.astype(jnp.bfloat16), inter_out, preferred_element_type=jnp.float32
        )
        spectrum_now = wet_factor * (turned + source.reshape(spectrum_now.shape))
    profile = jnp.tile(lax.dynamic_slice_in_dim(drift_weights, band_index * NFL, NFL, 1), (1, ND))
    final_flat = spectrum_now.reshape(-1, bin_count)
    contract = (((1,), (1,)), ((), ()))
    part_x = lax.dot_general(
        final_flat,
        profile * cosine,
        contract,
        precision=highest,
        preferred_element_type=jnp.float32,
    )
    part_y = lax.dot_general(
        final_flat,
        profile * sine_value,
        contract,
        precision=highest,
        preferred_element_type=jnp.float32,
    )
    drift_x, drift_y = (
        lax.psum_scatter(part_x, "grp", scatter_dimension=1, tiled=True),
        lax.psum_scatter(part_y, "grp", scatter_dimension=1, tiled=True),
    )
    drift_x = drift_x.reshape(tile_x, tile_y, levels_own)
    drift_y = drift_y.reshape(tile_x, tile_y, levels_own)
    velocity_u = ocean_u
    velocity_v = ocean_v
    for repeat in range(OCEAN_SECTIONS):
        stacked = jnp.concatenate([velocity_u, velocity_v], axis=2)
        padded = extended(stacked, (("gx", 0), ("gy", 1)), 1)
        laplace_both = (
            padded[2:, 1:-1]
            + padded[:-2, 1:-1]
            + padded[1:-1, 2:]
            + padded[1:-1, :-2]
            - 4.0 * stacked
        )
        laplace_u = laplace_both[:, :, :levels_own]
        laplace_v = laplace_both[:, :, levels_own:]
        first_u = velocity_u + ocean_step * (
            coriolis * (velocity_v + drift_y) + viscosity * laplace_u
        )
        first_v = velocity_v + ocean_step * (
            -coriolis * (velocity_u + drift_x) + viscosity * laplace_v
        )
        whole_u, whole_v = (
            lax.all_gather(first_u, "grp", axis=2, tiled=True),
            lax.all_gather(first_v, "grp", axis=2, tiled=True),
        )
        velocity_u = wet_factor * (
            first_u + jnp.einsum("abk,kl->abl", whole_u, mixing, precision=highest)
        )
        velocity_v = wet_factor * (
            first_v + jnp.einsum("abk,kl->abl", whole_v, mixing, precision=highest)
        )
    return (spectrum_now, velocity_u, velocity_v, drift_x, drift_y)


def solution(mesh):
    in_specs = (
        P("gx", "gy", "grp"),
        P("gx", "gy"),
        P("gx", "gy"),
        P("gx", "gy", "grp"),
        P("gx", "gy", "grp"),
        P(),
        P(),
        P("grp", None),
        P("grp", None),
        P(None, "grp"),
        P(None, "grp"),
    )
    out_specs = (
        P("gx", "gy", "grp"),
        P("gx", "gy", "grp"),
        P("gx", "gy", "grp"),
        P("gx", "gy", "grp"),
        P("gx", "gy", "grp"),
    )
    return jax.shard_map(body, mesh=mesh, in_specs=in_specs, out_specs=out_specs, check_vma=False)
```

profile of v0, /device:TPU:24, one launch (start us, length us, event | category | flops | bytes accessed | tf_op | source)
XLA Modules:
  0.0 159.7 jit_solution(4556036495489061007)
XLA Ops:
  0.7 0.7 copy-done.29
  1.5 4.5 %all_gather.18 = f32[2,48,40]{1,0,2:T(2,128)S(1)} all-gather(f32[2,48,20]{1,0,2:T(2,128)S(1)} %copy-done.17), channel_id=1, replica_groups=mesh['grp'=2,'gx'=8,'gy'=2] {'grp'}, dimensions={2}, use_global_device_ids=true | all-gather | bytes 23040 | tf_op jit(solution)/shard_map/all_gather | solution.py:81
  7.1 0.7 copy-done.18
  7.8 4.4 %all_gather.19 = f32[2,48,40]{1,0,2:T(2,128)S(1)} all-gather(f32[2,48,20]{1,0,2:T(2,128)S(1)} %copy-done.18), channel_id=1, replica_groups=mesh['grp'=2,'gx'=8,'gy'=2] {'grp'}, dimensions={2}, use_global_device_ids=true | all-gather | bytes 23040 | tf_op jit(solution)/shard_map/all_gather | solution.py:82
  13.4 3.4 %collective-permute-start.4 = (f32[2,48,32]{1,0,2:T(2,128)S(1)}, f32[2,48,32]{1,0,2:T(2,128)}, u32[]{:S(2)}, u32[]{:S(2)}) collective-permute-start(f32[2,48,32]{1,0,2:T(2,128)S(1)} %constant_dynamic-update-slice_fusion), channel_id=1, source_target_pairs={{0,2},{2,4},{4,6},{6,8},{8,10},{10,12},{12,14},{1,3},{3,5},{5,7},{... | collective-permute-start | bytes 36872 | tf_op jit(solution)/shard_map/ppermute | solution.py:26
  16.8 3.3 %collective-permute-start.5 = (f32[2,48,32]{1,0,2:T(2,128)S(1)}, f32[2,48,32]{1,0,2:T(2,128)}, u32[]{:S(2)}, u32[]{:S(2)}) collective-permute-start(f32[2,48,32]{1,0,2:T(2,128)S(1)} %constant_dynamic-update-slice_fusion), channel_id=1, source_target_pairs={{2,0},{4,2},{6,4},{8,6},{10,8},{12,10},{14,12},{3,1},{5,3},{7,5},{... | collective-permute-start | bytes 36872 | tf_op jit(solution)/shard_map/ppermute | solution.py:27
  20.7 3.2 %collective-permute-start = (f32[2,48,576]{2,1,0:T(8,128)S(1)}, f32[2,48,576]{2,1,0:T(8,128)S(1)}, u32[]{:S(2)}, u32[]{:S(2)}) collective-permute-start(f32[2,48,576]{2,1,0:T(8,128)S(1)} %get-tuple-element.49), channel_id=1, source_target_pairs={{0,2},{2,4},{4,6},{6,8},{8,10},{10,12},{12,14},{1,3},{3,5},{5,7},{... | collective-permute-start | bytes 663560 | tf_op jit(solution)/shard_map/ppermute | solution.py:26
  24.6 3.6 %collective-permute-start.16 = (f32[1,48,40]{1,2,0:T(8,128)}, f32[1,48,40]{1,2,0:T(8,128)}, u32[]{:S(2)}, u32[]{:S(2)}) collective-permute-start(f32[1,48,40]{1,2,0:T(8,128)} %get-tuple-element.81), channel_id=1, source_target_pairs={{2,0},{4,2},{6,4},{8,6},{10,8},{12,10},{14,12},{3,1},{5,3},{7,5},{... | collective-permute-start | bytes 23048 | tf_op jit(solution)/shard_map/ppermute | solution.py:27
  28.2 2.8 %collective-permute-start.17 = (f32[1,48,40]{1,2,0:T(8,128)}, f32[1,48,40]{1,2,0:T(8,128)}, u32[]{:S(2)}, u32[]{:S(2)}) collective-permute-start(f32[1,48,40]{1,2,0:T(8,128)} %get-tuple-element.80), channel_id=1, source_target_pairs={{0,2},{2,4},{4,6},{6,8},{8,10},{10,12},{12,14},{1,3},{3,5},{5,7},{... | collective-permute-start | bytes 23048 | tf_op jit(solution)/shard_map/ppermute | solution.py:26
  31.0 0.6 fusion.98
  31.6 0.6 fusion.92
  32.7 1.2 convolution_multiply_fusion.2
  33.9 0.9 broadcast_multiply_fusion
  35.7 0.8 pad_maximum_fusion.4
  36.4 0.7 fusion.117
  37.1 1.3 collective-permute-start.18
  38.4 4.3 %collective-permute-start.19 = (f32[4,1,40]{1,2,0:T(8,128)}, f32[4,1,40]{1,2,0:T(8,128)}, u32[]{:S(2)}, u32[]{:S(2)}) collective-permute-start(f32[4,1,40]{1,2,0:T(8,128)} %get-tuple-element.77), channel_id=1, source_target_pairs={{0,1},{2,3},{4,5},{6,7},{8,9},{10,11},{12,13},{14,15},{16,17},{18,... | collective-permute-start | bytes 1928 | tf_op jit(solution)/shard_map/ppermute | solution.py:26
  42.7 0.9 copy.297
  43.6 0.7 copy-done.30
  45.5 4.0 %collective-permute-start.1 = (f32[2,48,576]{2,1,0:T(8,128)S(1)}, f32[2,48,576]{2,1,0:T(8,128)S(1)}, u32[]{:S(2)}, u32[]{:S(2)}) collective-permute-start(f32[2,48,576]{2,1,0:T(8,128)S(1)} %get-tuple-element.49), channel_id=1, source_target_pairs={{2,0},{4,2},{6,4},{8,6},{10,8},{12,10},{14,12},{3,1},{5,3},{7,5},{... | collective-permute-start | bytes 663560 | tf_op jit(solution)/shard_map/ppermute | solution.py:27
  49.5 0.9 fusion.41
  50.5 0.8 pad_maximum_fusion.3
  51.4 1.3 collective-permute-start.6
  52.7 1.3 collective-permute-start.7
  54.1 0.7 pad_maximum_fusion.40
  54.9 3.6 %collective-permute-start.2 = (f32[6,2,576]{2,1,0:T(2,128)}, f32[6,2,576]{2,1,0:T(2,128)}, u32[]{:S(2)}, u32[]{:S(2)}) collective-permute-start(f32[6,2,576]{2,1,0:T(2,128)} %get-tuple-element.54), channel_id=1, source_target_pairs={{0,1},{2,3},{4,5},{6,7},{8,9},{10,11},{12,13},{14,15},{16,17},{18,... | collective-permute-start | bytes 82952 | tf_op jit(solution)/shard_map/ppermute | solution.py:26
  58.5 1.3 collective-permute-start.3
  59.8 0.9 pad_maximum_fusion.41
  61.0 0.9 collective-permute-done.3
  61.9 1.2 pad_maximum_fusion
  64.3 0.7 copy-done.11
  65.3 1.9 %collective-permute-start.8 = (f32[2,48,576]{2,1,0:T(8,128)S(1)}, f32[2,48,576]{2,1,0:T(8,128)S(1)}, u32[]{:S(2)}, u32[]{:S(2)}) collective-permute-start(f32[2,48,576]{2,1,0:T(8,128)S(1)} %get-tuple-element.46), channel_id=1, source_target_pairs={{0,2},{2,4},{4,6},{6,8},{8,10},{10,12},{12,14},{1,3},{3,5},{5,7},{... | collective-permute-start | bytes 663560 | tf_op jit(solution)/shard_map/ppermute | solution.py:26
  67.2 4.8 %collective-permute-start.9 = (f32[2,48,576]{2,1,0:T(8,128)S(1)}, f32[2,48,576]{2,1,0:T(8,128)S(1)}, u32[]{:S(2)}, u32[]{:S(2)}) collective-permute-start(f32[2,48,576]{2,1,0:T(8,128)S(1)} %get-tuple-element.46), channel_id=1, source_target_pairs={{2,0},{4,2},{6,4},{8,6},{10,8},{12,10},{14,12},{3,1},{5,3},{7,5},{... | collective-permute-start | bytes 663560 | tf_op jit(solution)/shard_map/ppermute | solution.py:27
  72.0 0.9 fusion.119
  73.0 3.9 %collective-permute-done.8 = f32[2,48,576]{2,1,0:T(8,128)S(1)} collective-permute-done((f32[2,48,576]{2,1,0:T(8,128)S(1)}, f32[2,48,576]{2,1,0:T(8,128)S(1)}, u32[]{:S(2)}, u32[]{:S(2)}) %collective-permute-start.8) | collective-permute-done | bytes 221216 | tf_op jit(solution)/shard_map/ppermute | solution.py:26
  76.8 5.2 %collective-permute-done.9 = f32[2,48,576]{2,1,0:T(8,128)S(1)} collective-permute-done((f32[2,48,576]{2,1,0:T(8,128)S(1)}, f32[2,48,576]{2,1,0:T(8,128)S(1)}, u32[]{:S(2)}, u32[]{:S(2)}) %collective-permute-start.9) | collective-permute-done | bytes 221216 | tf_op jit(solution)/shard_map/ppermute | solution.py:27
  82.0 0.7 pad_maximum_fusion.37
  82.7 2.6 %collective-permute-start.10 = (f32[6,2,576]{2,1,0:T(2,128)}, f32[6,2,576]{2,1,0:T(2,128)}, u32[]{:S(2)}, u32[]{:S(2)}) collective-permute-start(f32[6,2,576]{2,1,0:T(2,128)} %get-tuple-element.52), channel_id=1, source_target_pairs={{0,1},{2,3},{4,5},{6,7},{8,9},{10,11},{12,13},{14,15},{16,17},{18,... | collective-permute-start | bytes 82952 | tf_op jit(solution)/shard_map/ppermute | solution.py:26
  85.3 1.3 collective-permute-start.11
  86.6 2.1 %convolution_multiply_fusion.1 = f32[96,576]{1,0:T(8,128)} fusion(bf16[512,576]{0,1:T(8,128)(2,1)S(1)} %copy-done, f32[96,512]{1,0:T(8,128)} %fusion.119, bf16[96,576]{1,0:T(8,128)(2,1)S(1)} %bitcast.65, bf16[576,512]{1,0:T(8,128)(2,1)S(1)} %copy-done.2), kind=kOutput, calls=%fused_computation.3 | convolution fusion | flops 113399808 | bytes 1708032 | tf_op jit(solution)/shard_map/dot_general | solution.py:110
  88.7 1.1 pad_maximum_fusion.1
  90.4 0.7 copy-done.10
  91.3 1.9 %collective-permute-start.12 = (f32[2,48,576]{2,1,0:T(8,128)S(1)}, f32[2,48,576]{2,1,0:T(8,128)S(1)}, u32[]{:S(2)}, u32[]{:S(2)}) collective-permute-start(f32[2,48,576]{2,1,0:T(8,128)S(1)} %get-tuple-element.44), channel_id=1, source_target_pairs={{0,2},{2,4},{4,6},{6,8},{8,10},{10,12},{12,14},{1,3},{3,5},{5,7},{... | collective-permute-start | bytes 663560 | tf_op jit(solution)/shard_map/ppermute | solution.py:26
  93.2 4.8 %collective-permute-start.13 = (f32[2,48,576]{2,1,0:T(8,128)S(1)}, f32[2,48,576]{2,1,0:T(8,128)S(1)}, u32[]{:S(2)}, u32[]{:S(2)}) collective-permute-start(f32[2,48,576]{2,1,0:T(8,128)S(1)} %get-tuple-element.44), channel_id=1, source_target_pairs={{2,0},{4,2},{6,4},{8,6},{10,8},{12,10},{14,12},{3,1},{5,3},{7,5},{... | collective-permute-start | bytes 663560 | tf_op jit(solution)/shard_map/ppermute | solution.py:27
  98.1 0.9 fusion.120
  99.0 3.3 %collective-permute-done.12 = f32[2,48,576]{2,1,0:T(8,128)S(1)} collective-permute-done((f32[2,48,576]{2,1,0:T(8,128)S(1)}, f32[2,48,576]{2,1,0:T(8,128)S(1)}, u32[]{:S(2)}, u32[]{:S(2)}) %collective-permute-start.12) | collective-permute-done | bytes 221216 | tf_op jit(solution)/shard_map/ppermute | solution.py:26
  102.3 5.8 %collective-permute-done.13 = f32[2,48,576]{2,1,0:T(8,128)S(1)} collective-permute-done((f32[2,48,576]{2,1,0:T(8,128)S(1)}, f32[2,48,576]{2,1,0:T(8,128)S(1)}, u32[]{:S(2)}, u32[]{:S(2)}) %collective-permute-start.13) | collective-permute-done | bytes 221216 | tf_op jit(solution)/shard_map/ppermute | solution.py:27
  108.1 0.7 pad_maximum_fusion.34
  108.8 2.0 %collective-permute-start.14 = (f32[6,2,576]{2,1,0:T(2,128)}, f32[6,2,576]{2,1,0:T(2,128)S(1)}, u32[]{:S(2)}, u32[]{:S(2)}) collective-permute-start(f32[6,2,576]{2,1,0:T(2,128)} %get-tuple-element.50), channel_id=1, source_target_pairs={{0,1},{2,3},{4,5},{6,7},{8,9},{10,11},{12,13},{14,15},{16,17},{18,... | collective-permute-start | bytes 82952 | tf_op jit(solution)/shard_map/ppermute | solution.py:26
  110.9 1.4 collective-permute-start.15
  112.3 1.4 convolution_multiply_fusion
  115.0 0.8 copy-done.4
  116.4 0.6 fusion.121
  117.1 8.5 %all-reduce.2 = (f32[96,40]{0,1:T(8,128)S(1)}, f32[96,40]{0,1:T(8,128)S(1)}) all-reduce(f32[96,40]{0,1:T(8,128)S(1)} %fusion.121, f32[96,40]{0,1:T(8,128)S(1)} %fusion.122), channel_id=2, replica_groups=mesh['grp'=2,'gx'=8,'gy'=2] {'grp'}, use_global_device_ids=true, to_apply=%region_0.2.clone | all-reduce | flops 7680 | bytes 61440
  125.9 4.5 %all_gather.20 = f32[2,48,40]{1,0,2:T(2,128)S(1)} all-gather(f32[2,48,20]{1,0,2:T(2,128)S(1)} %copy.304), channel_id=1, replica_groups=mesh['grp'=2,'gx'=8,'gy'=2] {'grp'}, dimensions={2}, use_global_device_ids=true | all-gather | bytes 23040 | tf_op jit(solution)/shard_map/all_gather | solution.py:158
  130.3 4.5 %all_gather.21 = f32[2,48,40]{1,0,2:T(2,128)S(1)} all-gather(f32[2,48,20]{1,0,2:T(2,128)S(1)} %copy.309), channel_id=1, replica_groups=mesh['grp'=2,'gx'=8,'gy'=2] {'grp'}, dimensions={2}, use_global_device_ids=true | all-gather | bytes 23040 | tf_op jit(solution)/shard_map/all_gather | solution.py:159
  135.2 1.9 %collective-permute-start.20 = (f32[1,48,40]{1,2,0:T(8,128)S(1)}, f32[1,48,40]{1,2,0:T(8,128)S(1)}, u32[]{:S(2)}, u32[]{:S(2)}) collective-permute-start(f32[1,48,40]{1,2,0:T(8,128)S(1)} %get-tuple-element.79), channel_id=1, source_target_pairs={{2,0},{4,2},{6,4},{8,6},{10,8},{12,10},{14,12},{3,1},{5,3},{7,5},{... | collective-permute-start | bytes 23048 | tf_op jit(solution)/shard_map/ppermute | solution.py:27
  137.1 3.9 %collective-permute-start.21 = (f32[1,48,40]{1,2,0:T(8,128)S(1)}, f32[1,48,40]{1,2,0:T(8,128)S(1)}, u32[]{:S(2)}, u32[]{:S(2)}) collective-permute-start(f32[1,48,40]{1,2,0:T(8,128)S(1)} %get-tuple-element.78), channel_id=1, source_target_pairs={{0,2},{2,4},{4,6},{6,8},{8,10},{10,12},{12,14},{1,3},{3,5},{5,7},{... | collective-permute-start | bytes 23048 | tf_op jit(solution)/shard_map/ppermute | solution.py:26
  141.0 2.6 %collective-permute-done.21 = f32[1,48,40]{1,2,0:T(8,128)S(1)} collective-permute-done((f32[1,48,40]{1,2,0:T(8,128)S(1)}, f32[1,48,40]{1,2,0:T(8,128)S(1)}, u32[]{:S(2)}, u32[]{:S(2)}) %collective-permute-start.21) | collective-permute-done | bytes 7712 | tf_op jit(solution)/shard_map/ppermute | solution.py:26
  143.8 1.3 collective-permute-start.22
  145.1 3.0 %collective-permute-start.23 = (f32[4,1,40]{1,2,0:T(8,128)S(1)}, f32[4,1,40]{1,2,0:T(8,128)S(1)}, u32[]{:S(2)}, u32[]{:S(2)}) collective-permute-start(f32[4,1,40]{1,2,0:T(8,128)S(1)} %get-tuple-element.73), channel_id=1, source_target_pairs={{0,1},{2,3},{4,5},{6,7},{8,9},{10,11},{12,13},{14,15},{16,17},{18,... | collective-permute-start | bytes 1928 | tf_op jit(solution)/shard_map/ppermute | solution.py:26
  148.1 0.9 collective-permute-done.23
  149.2 4.5 %all_gather.23 = f32[2,48,40]{1,0,2:T(2,128)S(1)} all-gather(f32[2,48,20]{1,0,2:T(2,128)S(1)} %copy.315), channel_id=1, replica_groups=mesh['grp'=2,'gx'=8,'gy'=2] {'grp'}, dimensions={2}, use_global_device_ids=true | all-gather | bytes 23040 | tf_op jit(solution)/shard_map/all_gather | solution.py:159
  154.4 4.5 %all_gather.22 = f32[2,48,40]{1,0,2:T(2,128)S(1)} all-gather(f32[2,48,20]{1,0,2:T(2,128)S(1)} %copy.312), channel_id=1, replica_groups=mesh['grp'=2,'gx'=8,'gy'=2] {'grp'}, dimensions={2}, use_global_device_ids=true | all-gather | bytes 23040 | tf_op jit(solution)/shard_map/all_gather | solution.py:158
  (143 shorter events, 12.3 us)
Async XLA Ops:
  0.6 32.0 %copy-start = (bf16[512,576]{0,1:T(8,128)(2,1)S(1)}, bf16[512,576]{0,1:T(8,128)(2,1)}, u32[]{:S(2)}) copy-start(bf16[512,576]{0,1:T(8,128)(2,1)} %param.22) | copy-start | bytes 1769476
  0.6 0.7 copy-start.29
  0.7 0.8 copy-start.17
  6.0 0.7 copy-start.26
  7.1 0.8 copy-start.18
  12.4 7.8 %copy-start.28 = (s32[2,48]{1,0:T(2,128)S(1)}, s32[2,48]{1,0:T(2,128)}, u32[]{:S(2)}) copy-start(s32[2,48]{1,0:T(2,128)} %param.14) | copy-start | bytes 1156
  12.4 7.8 %copy-start.13 = (f32[2,48,576]{2,1,0:T(8,128)S(1)}, f32[2,48,576]{2,1,0:T(8,128)}, u32[]{:S(2)}) copy-start(f32[2,48,576]{2,1,0:T(8,128)} %param.13) | copy-start | bytes 663556
  13.0 19.4 %copy-start.1 = (bf16[576,512]{1,0:T(8,128)(2,1)S(1)}, bf16[576,512]{1,0:T(8,128)(2,1)}, u32[]{:S(2)}) copy-start(bf16[576,512]{1,0:T(8,128)(2,1)} %param.20) | copy-start | bytes 1769476
  13.4 37.1 %collective-permute-start.4 = (f32[2,48,32]{1,0,2:T(2,128)S(1)}, f32[2,48,32]{1,0,2:T(2,128)}, u32[]{:S(2)}, u32[]{:S(2)}) collective-permute-start(f32[2,48,32]{1,0,2:T(2,128)S(1)} %constant_dynamic-update-slice_fusion), channel_id=1, source_target_pairs={{0,2},{2,4},{4,6},{6,8},{8,10},{10,12},{12,14},{1,3},{3,5},{5,7},{... | collective-permute-start | bytes 36872 | tf_op jit(solution)/shard_map/ppermute | solution.py:26
  16.8 33.7 %collective-permute-start.5 = (f32[2,48,32]{1,0,2:T(2,128)S(1)}, f32[2,48,32]{1,0,2:T(2,128)}, u32[]{:S(2)}, u32[]{:S(2)}) collective-permute-start(f32[2,48,32]{1,0,2:T(2,128)S(1)} %constant_dynamic-update-slice_fusion), channel_id=1, source_target_pairs={{2,0},{4,2},{6,4},{8,6},{10,8},{12,10},{14,12},{3,1},{5,3},{7,5},{... | collective-permute-start | bytes 36872 | tf_op jit(solution)/shard_map/ppermute | solution.py:27
  20.2 0.5 copy-start.19
  20.2 12.2 %copy-start.27 = (f32[40,32]{0,1:T(8,128)S(1)}, f32[40,32]{0,1:T(8,128)}, u32[]{:S(2)}) copy-start(f32[40,32]{0,1:T(8,128)} %param.19) | copy-start | bytes 15364
  20.7 12.0 %copy-start.2 = (bf16[576,512]{1,0:T(8,128)(2,1)S(1)}, bf16[576,512]{1,0:T(8,128)(2,1)}, u32[]{:S(2)}) copy-start(bf16[576,512]{1,0:T(8,128)(2,1)} %param.21) | copy-start | bytes 1769476
  20.7 33.3 %collective-permute-start = (f32[2,48,576]{2,1,0:T(8,128)S(1)}, f32[2,48,576]{2,1,0:T(8,128)S(1)}, u32[]{:S(2)}, u32[]{:S(2)}) collective-permute-start(f32[2,48,576]{2,1,0:T(8,128)S(1)} %get-tuple-element.49), channel_id=1, source_target_pairs={{0,2},{2,4},{4,6},{6,8},{8,10},{10,12},{12,14},{1,3},{3,5},{5,7},{... | collective-permute-start | bytes 663560 | tf_op jit(solution)/shard_map/ppermute | solution.py:26
  24.6 11.1 %collective-permute-start.16 = (f32[1,48,40]{1,2,0:T(8,128)}, f32[1,48,40]{1,2,0:T(8,128)}, u32[]{:S(2)}, u32[]{:S(2)}) collective-permute-start(f32[1,48,40]{1,2,0:T(8,128)} %get-tuple-element.81), channel_id=1, source_target_pairs={{2,0},{4,2},{6,4},{8,6},{10,8},{12,10},{14,12},{3,1},{5,3},{7,5},{... | collective-permute-start | bytes 23048 | tf_op jit(solution)/shard_map/ppermute | solution.py:27
  28.2 7.4 %collective-permute-start.17 = (f32[1,48,40]{1,2,0:T(8,128)}, f32[1,48,40]{1,2,0:T(8,128)}, u32[]{:S(2)}, u32[]{:S(2)}) collective-permute-start(f32[1,48,40]{1,2,0:T(8,128)} %get-tuple-element.80), channel_id=1, source_target_pairs={{0,2},{2,4},{4,6},{6,8},{8,10},{10,12},{12,14},{1,3},{3,5},{5,7},{... | collective-permute-start | bytes 23048 | tf_op jit(solution)/shard_map/ppermute | solution.py:26
  37.1 8.4 %collective-permute-start.18 = (f32[4,1,40]{1,2,0:T(8,128)}, f32[4,1,40]{1,2,0:T(8,128)}, u32[]{:S(2)}, u32[]{:S(2)}) collective-permute-start(f32[4,1,40]{1,2,0:T(8,128)} %get-tuple-element.76), channel_id=1, source_target_pairs={{1,0},{3,2},{5,4},{7,6},{9,8},{11,10},{13,12},{15,14},{17,16},{19,... | collective-permute-start | bytes 1928 | tf_op jit(solution)/shard_map/ppermute | solution.py:27
  38.4 11.1 %collective-permute-start.19 = (f32[4,1,40]{1,2,0:T(8,128)}, f32[4,1,40]{1,2,0:T(8,128)}, u32[]{:S(2)}, u32[]{:S(2)}) collective-permute-start(f32[4,1,40]{1,2,0:T(8,128)} %get-tuple-element.77), channel_id=1, source_target_pairs={{0,1},{2,3},{4,5},{6,7},{8,9},{10,11},{12,13},{14,15},{16,17},{18,... | collective-permute-start | bytes 1928 | tf_op jit(solution)/shard_map/ppermute | solution.py:26
  43.6 0.7 copy-start.30
  45.5 8.5 %collective-permute-start.1 = (f32[2,48,576]{2,1,0:T(8,128)S(1)}, f32[2,48,576]{2,1,0:T(8,128)S(1)}, u32[]{:S(2)}, u32[]{:S(2)}) collective-permute-start(f32[2,48,576]{2,1,0:T(8,128)S(1)} %get-tuple-element.49), channel_id=1, source_target_pairs={{2,0},{4,2},{6,4},{8,6},{10,8},{12,10},{14,12},{3,1},{5,3},{7,5},{... | collective-permute-start | bytes 663560 | tf_op jit(solution)/shard_map/ppermute | solution.py:27
  51.4 8.3 %collective-permute-start.6 = (f32[6,2,32]{1,0,2:T(8,128)S(1)}, f32[6,2,32]{1,0,2:T(8,128)S(1)}, u32[]{:S(2)}, u32[]{:S(2)}) collective-permute-start(f32[6,2,32]{1,0,2:T(8,128)S(1)} %get-tuple-element.68), channel_id=1, source_target_pairs={{0,1},{2,3},{4,5},{6,7},{8,9},{10,11},{12,13},{14,15},{16,17},{18,... | collective-permute-start | bytes 4616 | tf_op jit(solution)/shard_map/ppermute | solution.py:26
  52.7 7.0 %collective-permute-start.7 = (f32[6,2,32]{1,0,2:T(8,128)S(1)}, f32[6,2,32]{1,0,2:T(8,128)S(1)}, u32[]{:S(2)}, u32[]{:S(2)}) collective-permute-start(f32[6,2,32]{1,0,2:T(8,128)S(1)} %get-tuple-element.69), channel_id=1, source_target_pairs={{1,0},{3,2},{5,4},{7,6},{9,8},{11,10},{13,12},{15,14},{17,16},{19,... | collective-permute-start | bytes 4616 | tf_op jit(solution)/shard_map/ppermute | solution.py:27
  54.1 0.8 copy-start.5
  54.1 0.8 copy-start.6
  54.9 6.1 %collective-permute-start.2 = (f32[6,2,576]{2,1,0:T(2,128)}, f32[6,2,576]{2,1,0:T(2,128)}, u32[]{:S(2)}, u32[]{:S(2)}) collective-permute-start(f32[6,2,576]{2,1,0:T(2,128)} %get-tuple-element.54), channel_id=1, source_target_pairs={{0,1},{2,3},{4,5},{6,7},{8,9},{10,11},{12,13},{14,15},{16,17},{18,... | collective-permute-start | bytes 82952 | tf_op jit(solution)/shard_map/ppermute | solution.py:26
  58.5 3.4 %collective-permute-start.3 = (f32[6,2,576]{2,1,0:T(2,128)}, f32[6,2,576]{2,1,0:T(2,128)}, u32[]{:S(2)}, u32[]{:S(2)}) collective-permute-start(f32[6,2,576]{2,1,0:T(2,128)} %get-tuple-element.55), channel_id=1, source_target_pairs={{1,0},{3,2},{5,4},{7,6},{9,8},{11,10},{13,12},{15,14},{17,16},{19,... | collective-permute-start | bytes 82952 | tf_op jit(solution)/shard_map/ppermute | solution.py:27
  61.9 1.2 copy-start.22
  63.1 0.7 copy-start.21
  64.0 0.9 copy-start.11
  64.0 1.1 copy-start.12
  64.3 0.8 copy-start.25
  64.3 0.8 copy-start.24
  64.3 0.8 copy-start.23
  64.3 0.8 copy-start.20
  65.3 11.5 %collective-permute-start.8 = (f32[2,48,576]{2,1,0:T(8,128)S(1)}, f32[2,48,576]{2,1,0:T(8,128)S(1)}, u32[]{:S(2)}, u32[]{:S(2)}) collective-permute-start(f32[2,48,576]{2,1,0:T(8,128)S(1)} %get-tuple-element.46), channel_id=1, source_target_pairs={{0,2},{2,4},{4,6},{6,8},{8,10},{10,12},{12,14},{1,3},{3,5},{5,7},{... | collective-permute-start | bytes 663560 | tf_op jit(solution)/shard_map/ppermute | solution.py:26
  67.2 14.8 %collective-permute-start.9 = (f32[2,48,576]{2,1,0:T(8,128)S(1)}, f32[2,48,576]{2,1,0:T(8,128)S(1)}, u32[]{:S(2)}, u32[]{:S(2)}) collective-permute-start(f32[2,48,576]{2,1,0:T(8,128)S(1)} %get-tuple-element.46), channel_id=1, source_target_pairs={{2,0},{4,2},{6,4},{8,6},{10,8},{12,10},{14,12},{3,1},{5,3},{7,5},{... | collective-permute-start | bytes 663560 | tf_op jit(solution)/shard_map/ppermute | solution.py:27
  82.0 0.7 copy-start.9
  82.7 6.0 %collective-permute-start.10 = (f32[6,2,576]{2,1,0:T(2,128)}, f32[6,2,576]{2,1,0:T(2,128)}, u32[]{:S(2)}, u32[]{:S(2)}) collective-permute-start(f32[6,2,576]{2,1,0:T(2,128)} %get-tuple-element.52), channel_id=1, source_target_pairs={{0,1},{2,3},{4,5},{6,7},{8,9},{10,11},{12,13},{14,15},{16,17},{18,... | collective-permute-start | bytes 82952 | tf_op jit(solution)/shard_map/ppermute | solution.py:26
  85.3 3.4 %collective-permute-start.11 = (f32[6,2,576]{2,1,0:T(2,128)}, f32[6,2,576]{2,1,0:T(2,128)}, u32[]{:S(2)}, u32[]{:S(2)}) collective-permute-start(f32[6,2,576]{2,1,0:T(2,128)} %get-tuple-element.53), channel_id=1, source_target_pairs={{1,0},{3,2},{5,4},{7,6},{9,8},{11,10},{13,12},{15,14},{17,16},{19,... | collective-permute-start | bytes 82952 | tf_op jit(solution)/shard_map/ppermute | solution.py:27
  90.2 0.9 copy-start.10
  91.3 11.0 %collective-permute-start.12 = (f32[2,48,576]{2,1,0:T(8,128)S(1)}, f32[2,48,576]{2,1,0:T(8,128)S(1)}, u32[]{:S(2)}, u32[]{:S(2)}) collective-permute-start(f32[2,48,576]{2,1,0:T(8,128)S(1)} %get-tuple-element.44), channel_id=1, source_target_pairs={{0,2},{2,4},{4,6},{6,8},{8,10},{10,12},{12,14},{1,3},{3,5},{5,7},{... | collective-permute-start | bytes 663560 | tf_op jit(solution)/shard_map/ppermute | solution.py:26
  93.2 14.9 %collective-permute-start.13 = (f32[2,48,576]{2,1,0:T(8,128)S(1)}, f32[2,48,576]{2,1,0:T(8,128)S(1)}, u32[]{:S(2)}, u32[]{:S(2)}) collective-permute-start(f32[2,48,576]{2,1,0:T(8,128)S(1)} %get-tuple-element.44), channel_id=1, source_target_pairs={{2,0},{4,2},{6,4},{8,6},{10,8},{12,10},{14,12},{3,1},{5,3},{7,5},{... | collective-permute-start | bytes 663560 | tf_op jit(solution)/shard_map/ppermute | solution.py:27
  108.1 0.7 copy-start.7
  108.8 4.9 %collective-permute-start.14 = (f32[6,2,576]{2,1,0:T(2,128)}, f32[6,2,576]{2,1,0:T(2,128)S(1)}, u32[]{:S(2)}, u32[]{:S(2)}) collective-permute-start(f32[6,2,576]{2,1,0:T(2,128)} %get-tuple-element.50), channel_id=1, source_target_pairs={{0,1},{2,3},{4,5},{6,7},{8,9},{10,11},{12,13},{14,15},{16,17},{18,... | collective-permute-start | bytes 82952 | tf_op jit(solution)/shard_map/ppermute | solution.py:26
  110.9 3.2 %copy-start.8 = (f32[2,48,576]{2,1,0:T(8,128)S(1)}, f32[2,48,576]{2,1,0:T(8,128)}, u32[]{:S(2)}) copy-start(f32[2,48,576]{2,1,0:T(8,128)} %copy-done.7) | copy-start | bytes 663556
  110.9 3.2 %collective-permute-start.15 = (f32[6,2,576]{2,1,0:T(2,128)S(1)}, f32[6,2,576]{2,1,0:T(2,128)S(1)}, u32[]{:S(2)}, u32[]{:S(2)}) collective-permute-start(f32[6,2,576]{2,1,0:T(2,128)S(1)} %get-tuple-element.51), channel_id=1, source_target_pairs={{1,0},{3,2},{5,4},{7,6},{9,8},{11,10},{13,12},{15,14},{17,16},{19,... | collective-permute-start | bytes 82952 | tf_op jit(solution)/shard_map/ppermute | solution.py:27
  114.8 1.0 copy-start.4
  115.0 1.4 copy-start.3
  125.7 23.4 %copy-start.15 = (f32[2,48,20]{1,0,2:T(2,128)}, f32[2,48,20]{1,0,2:T(2,128)S(1)}, u32[]{:S(2)}) copy-start(f32[2,48,20]{1,0,2:T(2,128)S(1)} %reshape.208) | copy-start | bytes 23044
  125.8 23.3 %copy-start.16 = (f32[2,48,20]{1,0,2:T(2,128)}, f32[2,48,20]{1,0,2:T(2,128)S(1)}, u32[]{:S(2)}) copy-start(f32[2,48,20]{1,0,2:T(2,128)S(1)} %reshape.209) | copy-start | bytes 23044
  130.3 4.5 %copy-start.14 = (f32[40,20]{0,1:T(8,128)S(1)}, f32[40,20]{0,1:T(8,128)}, u32[]{:S(2)}) copy-start(f32[40,20]{0,1:T(8,128)} %param.23) | copy-start | bytes 9604
  135.2 5.9 %collective-permute-start.20 = (f32[1,48,40]{1,2,0:T(8,128)S(1)}, f32[1,48,40]{1,2,0:T(8,128)S(1)}, u32[]{:S(2)}, u32[]{:S(2)}) collective-permute-start(f32[1,48,40]{1,2,0:T(8,128)S(1)} %get-tuple-element.79), channel_id=1, source_target_pairs={{2,0},{4,2},{6,4},{8,6},{10,8},{12,10},{14,12},{3,1},{5,3},{7,5},{... | collective-permute-start | bytes 23048 | tf_op jit(solution)/shard_map/ppermute | solution.py:27
  137.1 6.6 %collective-permute-start.21 = (f32[1,48,40]{1,2,0:T(8,128)S(1)}, f32[1,48,40]{1,2,0:T(8,128)S(1)}, u32[]{:S(2)}, u32[]{:S(2)}) collective-permute-start(f32[1,48,40]{1,2,0:T(8,128)S(1)} %get-tuple-element.78), channel_id=1, source_target_pairs={{0,2},{2,4},{4,6},{6,8},{8,10},{10,12},{12,14},{1,3},{3,5},{5,7},{... | collective-permute-start | bytes 23048 | tf_op jit(solution)/shard_map/ppermute | solution.py:26
  143.8 4.3 %collective-permute-start.22 = (f32[4,1,40]{1,2,0:T(8,128)S(1)}, f32[4,1,40]{1,2,0:T(8,128)S(1)}, u32[]{:S(2)}, u32[]{:S(2)}) collective-permute-start(f32[4,1,40]{1,2,0:T(8,128)S(1)} %get-tuple-element.72), channel_id=1, source_target_pairs={{1,0},{3,2},{5,4},{7,6},{9,8},{11,10},{13,12},{15,14},{17,16},{19,... | collective-permute-start | bytes 1928 | tf_op jit(solution)/shard_map/ppermute | solution.py:27
  145.1 3.9 %collective-permute-start.23 = (f32[4,1,40]{1,2,0:T(8,128)S(1)}, f32[4,1,40]{1,2,0:T(8,128)S(1)}, u32[]{:S(2)}, u32[]{:S(2)}) collective-permute-start(f32[4,1,40]{1,2,0:T(8,128)S(1)} %get-tuple-element.73), channel_id=1, source_target_pairs={{0,1},{2,3},{4,5},{6,7},{8,9},{10,11},{12,13},{14,15},{16,17},{18,... | collective-permute-start | bytes 1928 | tf_op jit(solution)/shard_map/ppermute | solution.py:26
where the time goes:
time: 161 us; the launch traced here: 160 us
  starting transfers between devices  64.3 us (40%)
  blocking collectives  35.2 us (22%)
  waiting for transfers between devices  23.1 us (14%)
  other arithmetic  13.4 us (8%)
  local copies, waits for them, and re-layouts  12.4 us (8%)
  matrix products  9.09 us (6%)
  between operations  2.19 us (1%)
    ppermute x12, starting transfers between devices, extended(): before = lax.ppermute(last, axis, up)  34 us
    ppermute x12, starting transfers between devices, extended(): after = lax.ppermute(leading, axis, down)  30.3 us
    ppermute x12, waiting for transfers between devices, extended(): after = lax.ppermute(leading, axis, down)  12.4 us
    ppermute x12, waiting for transfers between devices, extended(): before = lax.ppermute(last, axis, up)  10.7 us
    all_gather x2, blocking collectives, body(): lax.all_gather(first_u, 'grp', axis=2, tiled=True)  8.9 us
    all_gather x2, blocking collectives, body(): lax.all_gather(first_v, 'grp', axis=2, tiled=True)  8.9 us
    unnamed x1, blocking collectives  8.49 us
    unnamed x70, local copies, waits for them, and re-layouts  7.46 us
  transfers between devices with their start and end apart: 24, of which 8 were waited for; matrix products, arithmetic and copies ran while one was open for 11% of the time, Pallas kernels for 0%

commit v1 on v0

--- a/solution.py
+++ b/solution.py
@@ -14,6 +14,29 @@
 ocean_step = 0.4
 coriolis = 0.5
 viscosity = 0.1
+
+
+def laid_out(blocks, dim):
+    dims = list(blocks.shape[1:])
+    dims[dim] *= blocks.shape[0]
+    return jnp.moveaxis(blocks, 0, dim).reshape(dims)
+
+
+def collected_by_bits(x, axis):
+    size, index = (lax.axis_size(axis), lax.axis_index(axis))
+    blocks, bit = (x[None], 1)
+    while bit < size:
+        partner_block = lax.ppermute(blocks, axis, [(i, i ^ bit) for i in range(size)])
+        low = index & bit == 0
+        blocks = jnp.concatenate(
+            [jnp.where(low, blocks, partner_block), jnp.where(low, partner_block, blocks)]
+        )
+        bit *= 2
+    return blocks
+
+
+def collect(array, axis, dim):
+    return laid_out(collected_by_bits(array, axis), dim)
 
 
 def extended(array, sides, width):
@@ -156,7 +179,7 @@
         )
         whole_u, whole_v = (
             lax.all_gather(first_u, "grp", axis=2, tiled=True),
-            lax.all_gather(first_v, "grp", axis=2, tiled=True),
+            collect(first_v, "grp", 2),
         )
         velocity_u = wet_factor * (
             first_u + jnp.einsum("abk,kl->abl", whole_u, mixing, precision=highest)

time: 161 us -> 155 us (0.963)
  blocking collectives: 35.2 us -> 26.3 us
  waiting for transfers between devices: 23.1 us -> 26.9 us
    all_gather x2 -> x0, blocking collectives: 8.9 us -> none  [body(): lax.all_gather(first_v, 'grp', axis=2, tiled=True)]
    ppermute x0 -> x2, waiting for transfers between devices: none -> 3.12 us  [collected_by_bits(): lax.ppermute(blocks, axis, [(i, i ^ bit) for i in range(size)])]
    ppermute x12, starting transfers between devices: 34 us -> 32.1 us  [extended(): before = lax.ppermute(last, axis, up)]
  transfers between devices with their start and end apart: 24 -> 26, of which waited for: 8 -> 10; matrix products, arithmetic and copies ran while one was open for 11% -> 12% of each run, Pallas kernels for 0% -> 0%
where the time goes in v1:
time: 155 us; the launch traced here: 153 us
  starting transfers between devices  63.6 us (41%)
  waiting for transfers between devices  26.9 us (17%)
  blocking collectives  26.3 us (17%)
  other arithmetic  13.3 us (9%)
  local copies, waits for them, and re-layouts  11.8 us (8%)
  matrix products  9.14 us (6%)
  between operations  2.21 us (1%)
    ppermute x12, starting transfers between devices, extended(): before = lax.ppermute(last, axis, up)  32.1 us
    ppermute x12, starting transfers between devices, extended(): after = lax.ppermute(leading, axis, down)  30.3 us
    ppermute x12, waiting for transfers between devices, extended(): after = lax.ppermute(leading, axis, down)  13.1 us
    ppermute x12, waiting for transfers between devices, extended(): before = lax.ppermute(last, axis, up)  10.7 us
    all_gather x2, blocking collectives, body(): lax.all_gather(first_u, 'grp', axis=2, tiled=True)  8.9 us
    unnamed x1, blocking collectives  8.48 us
    unnamed x70, local copies, waits for them, and re-layouts  7.47 us
    concatenate x7, other arithmetic, extended(): array = jnp.concatenate([before, array, after], axis=dim)  4.84 us
  transfers between devices with their start and end apart: 26, of which 10 were waited for; matrix products, arithmetic and copies ran while one was open for 12% of the time, Pallas kernels for 0%

profile of v1, /device:TPU:24, one launch (start us, length us, event | category | flops | bytes accessed | tf_op | source)
XLA Modules:
  0.0 153.2 jit_solution(15306382402794167509)
XLA Ops:
  0.7 0.7 copy-done.29
  1.5 4.5 %all_gather.12 = f32[2,48,40]{1,0,2:T(2,128)S(1)} all-gather(f32[2,48,20]{1,0,2:T(2,128)S(1)} %copy-done.17), channel_id=1, replica_groups=mesh['grp'=2,'gx'=8,'gy'=2] {'grp'}, dimensions={2}, use_global_device_ids=true | all-gather | bytes 23040 | tf_op jit(solution)/shard_map/all_gather | solution.py:104
  7.1 0.7 copy-done.18
  7.9 4.4 %all_gather.13 = f32[2,48,40]{1,0,2:T(2,128)S(1)} all-gather(f32[2,48,20]{1,0,2:T(2,128)S(1)} %copy-done.18), channel_id=1, replica_groups=mesh['grp'=2,'gx'=8,'gy'=2] {'grp'}, dimensions={2}, use_global_device_ids=true | all-gather | bytes 23040 | tf_op jit(solution)/shard_map/all_gather | solution.py:105
  13.4 3.4 %collective-permute-start.4 = (f32[2,48,32]{1,0,2:T(2,128)S(1)}, f32[2,48,32]{1,0,2:T(2,128)}, u32[]{:S(2)}, u32[]{:S(2)}) collective-permute-start(f32[2,48,32]{1,0,2:T(2,128)S(1)} %constant_dynamic-update-slice_fusion), channel_id=1, source_target_pairs={{0,2},{2,4},{4,6},{6,8},{8,10},{10,12},{12,14},{1,3},{3,5},{5,7},{... | collective-permute-start | bytes 36872 | tf_op jit(solution)/shard_map/ppermute | solution.py:49
  16.8 3.3 %collective-permute-start.5 = (f32[2,48,32]{1,0,2:T(2,128)S(1)}, f32[2,48,32]{1,0,2:T(2,128)}, u32[]{:S(2)}, u32[]{:S(2)}) collective-permute-start(f32[2,48,32]{1,0,2:T(2,128)S(1)} %constant_dynamic-update-slice_fusion), channel_id=1, source_target_pairs={{2,0},{4,2},{6,4},{8,6},{10,8},{12,10},{14,12},{3,1},{5,3},{7,5},{... | collective-permute-start | bytes 36872 | tf_op jit(solution)/shard_map/ppermute | solution.py:50
  20.8 3.2 %collective-permute-start = (f32[2,48,576]{2,1,0:T(8,128)S(1)}, f32[2,48,576]{2,1,0:T(8,128)S(1)}, u32[]{:S(2)}, u32[]{:S(2)}) collective-permute-start(f32[2,48,576]{2,1,0:T(8,128)S(1)} %get-tuple-element.49), channel_id=1, source_target_pairs={{0,2},{2,4},{4,6},{6,8},{8,10},{10,12},{12,14},{1,3},{3,5},{5,7},{... | collective-permute-start | bytes 663560 | tf_op jit(solution)/shard_map/ppermute | solution.py:49
  24.6 3.6 %collective-permute-start.16 = (f32[1,48,40]{1,2,0:T(8,128)}, f32[1,48,40]{1,2,0:T(8,128)}, u32[]{:S(2)}, u32[]{:S(2)}) collective-permute-start(f32[1,48,40]{1,2,0:T(8,128)} %get-tuple-element.85), channel_id=1, source_target_pairs={{2,0},{4,2},{6,4},{8,6},{10,8},{12,10},{14,12},{3,1},{5,3},{7,5},{... | collective-permute-start | bytes 23048 | tf_op jit(solution)/shard_map/ppermute | solution.py:50
  28.3 2.8 %collective-permute-start.17 = (f32[1,48,40]{1,2,0:T(8,128)}, f32[1,48,40]{1,2,0:T(8,128)}, u32[]{:S(2)}, u32[]{:S(2)}) collective-permute-start(f32[1,48,40]{1,2,0:T(8,128)} %get-tuple-element.84), channel_id=1, source_target_pairs={{0,2},{2,4},{4,6},{6,8},{8,10},{10,12},{12,14},{1,3},{3,5},{5,7},{... | collective-permute-start | bytes 23048 | tf_op jit(solution)/shard_map/ppermute | solution.py:49
  31.0 0.6 fusion.98
  31.7 0.6 fusion.92
  32.7 1.2 convolution_multiply_fusion.2
  33.9 0.9 broadcast_multiply_fusion
  35.7 0.9 copy.305
  36.6 0.8 pad_maximum_fusion.4
  37.5 1.3 collective-permute-start.18
  38.8 3.0 %collective-permute-start.19 = (f32[4,1,40]{1,2,0:T(8,128)S(1)}, f32[4,1,40]{1,2,0:T(8,128)S(1)}, u32[]{:S(2)}, u32[]{:S(2)}) collective-permute-start(f32[4,1,40]{1,2,0:T(8,128)S(1)} %get-tuple-element.77), channel_id=1, source_target_pairs={{0,1},{2,3},{4,5},{6,7},{8,9},{10,11},{12,13},{14,15},{16,17},{18,... | collective-permute-start | bytes 1928 | tf_op jit(solution)/shard_map/ppermute | solution.py:49
  41.9 0.6 copy-done.30
  43.8 4.0 %collective-permute-start.1 = (f32[2,48,576]{2,1,0:T(8,128)S(1)}, f32[2,48,576]{2,1,0:T(8,128)S(1)}, u32[]{:S(2)}, u32[]{:S(2)}) collective-permute-start(f32[2,48,576]{2,1,0:T(8,128)S(1)} %get-tuple-element.49), channel_id=1, source_target_pairs={{2,0},{4,2},{6,4},{8,6},{10,8},{12,10},{14,12},{3,1},{5,3},{7,5},{... | collective-permute-start | bytes 663560 | tf_op jit(solution)/shard_map/ppermute | solution.py:50
  47.7 0.9 fusion.41
  48.6 0.8 pad_maximum_fusion.3
  49.6 1.3 collective-permute-start.6
  50.9 1.3 collective-permute-start.7
  52.2 0.7 collective-permute-done.1
  52.9 0.7 pad_maximum_fusion.40
  53.6 3.0 %collective-permute-start.2 = (f32[6,2,576]{2,1,0:T(2,128)}, f32[6,2,576]{2,1,0:T(2,128)}, u32[]{:S(2)}, u32[]{:S(2)}) collective-permute-start(f32[6,2,576]{2,1,0:T(2,128)} %get-tuple-element.54), channel_id=1, source_target_pairs={{0,1},{2,3},{4,5},{6,7},{8,9},{10,11},{12,13},{14,15},{16,17},{18,... | collective-permute-start | bytes 82952 | tf_op jit(solution)/shard_map/ppermute | solution.py:49
  56.6 1.3 collective-permute-start.3
  57.9 0.9 pad_maximum_fusion.41
  59.1 0.9 collective-permute-done.3
  60.1 1.2 pad_maximum_fusion
  62.4 0.7 copy-done.11
  63.4 1.9 %collective-permute-start.8 = (f32[2,48,576]{2,1,0:T(8,128)S(1)}, f32[2,48,576]{2,1,0:T(8,128)S(1)}, u32[]{:S(2)}, u32[]{:S(2)}) collective-permute-start(f32[2,48,576]{2,1,0:T(8,128)S(1)} %get-tuple-element.46), channel_id=1, source_target_pairs={{0,2},{2,4},{4,6},{6,8},{8,10},{10,12},{12,14},{1,3},{3,5},{5,7},{... | collective-permute-start | bytes 663560 | tf_op jit(solution)/shard_map/ppermute | solution.py:49
  65.4 4.8 %collective-permute-start.9 = (f32[2,48,576]{2,1,0:T(8,128)S(1)}, f32[2,48,576]{2,1,0:T(8,128)S(1)}, u32[]{:S(2)}, u32[]{:S(2)}) collective-permute-start(f32[2,48,576]{2,1,0:T(8,128)S(1)} %get-tuple-element.46), channel_id=1, source_target_pairs={{2,0},{4,2},{6,4},{8,6},{10,8},{12,10},{14,12},{3,1},{5,3},{7,5},{... | collective-permute-start | bytes 663560 | tf_op jit(solution)/shard_map/ppermute | solution.py:50
  70.2 0.9 fusion.119
  71.1 3.8 %collective-permute-done.8 = f32[2,48,576]{2,1,0:T(8,128)S(1)} collective-permute-done((f32[2,48,576]{2,1,0:T(8,128)S(1)}, f32[2,48,576]{2,1,0:T(8,128)S(1)}, u32[]{:S(2)}, u32[]{:S(2)}) %collective-permute-start.8) | collective-permute-done | bytes 221216 | tf_op jit(solution)/shard_map/ppermute | solution.py:49
  75.0 5.2 %collective-permute-done.9 = f32[2,48,576]{2,1,0:T(8,128)S(1)} collective-permute-done((f32[2,48,576]{2,1,0:T(8,128)S(1)}, f32[2,48,576]{2,1,0:T(8,128)S(1)}, u32[]{:S(2)}, u32[]{:S(2)}) %collective-permute-start.9) | collective-permute-done | bytes 221216 | tf_op jit(solution)/shard_map/ppermute | solution.py:50
  80.1 0.7 pad_maximum_fusion.37
  80.8 2.6 %collective-permute-start.10 = (f32[6,2,576]{2,1,0:T(2,128)}, f32[6,2,576]{2,1,0:T(2,128)}, u32[]{:S(2)}, u32[]{:S(2)}) collective-permute-start(f32[6,2,576]{2,1,0:T(2,128)} %get-tuple-element.52), channel_id=1, source_target_pairs={{0,1},{2,3},{4,5},{6,7},{8,9},{10,11},{12,13},{14,15},{16,17},{18,... | collective-permute-start | bytes 82952 | tf_op jit(solution)/shard_map/ppermute | solution.py:49
  83.4 1.3 collective-permute-start.11
  84.7 2.1 %convolution_multiply_fusion.1 = f32[96,576]{1,0:T(8,128)} fusion(bf16[512,576]{0,1:T(8,128)(2,1)S(1)} %copy-done, f32[96,512]{1,0:T(8,128)} %fusion.119, bf16[96,576]{1,0:T(8,128)(2,1)S(1)} %bitcast.77, bf16[576,512]{1,0:T(8,128)(2,1)S(1)} %copy-done.2), kind=kOutput, calls=%fused_computation.3 | convolution fusion | flops 113399808 | bytes 1708032 | tf_op jit(solution)/shard_map/dot_general | solution.py:133
  86.9 1.1 pad_maximum_fusion.1
  88.6 0.7 copy-done.10
  89.5 1.9 %collective-permute-start.12 = (f32[2,48,576]{2,1,0:T(8,128)S(1)}, f32[2,48,576]{2,1,0:T(8,128)S(1)}, u32[]{:S(2)}, u32[]{:S(2)}) collective-permute-start(f32[2,48,576]{2,1,0:T(8,128)S(1)} %get-tuple-element.44), channel_id=1, source_target_pairs={{0,2},{2,4},{4,6},{6,8},{8,10},{10,12},{12,14},{1,3},{3,5},{5,7},{... | collective-permute-start | bytes 663560 | tf_op jit(solution)/shard_map/ppermute | solution.py:49
  91.4 4.8 %collective-permute-start.13 = (f32[2,48,576]{2,1,0:T(8,128)S(1)}, f32[2,48,576]{2,1,0:T(8,128)S(1)}, u32[]{:S(2)}, u32[]{:S(2)}) collective-permute-start(f32[2,48,576]{2,1,0:T(8,128)S(1)} %get-tuple-element.44), channel_id=1, source_target_pairs={{2,0},{4,2},{6,4},{8,6},{10,8},{12,10},{14,12},{3,1},{5,3},{7,5},{... | collective-permute-start | bytes 663560 | tf_op jit(solution)/shard_map/ppermute | solution.py:50
  96.2 0.9 fusion.120
  97.2 3.3 %collective-permute-done.12 = f32[2,48,576]{2,1,0:T(8,128)S(1)} collective-permute-done((f32[2,48,576]{2,1,0:T(8,128)S(1)}, f32[2,48,576]{2,1,0:T(8,128)S(1)}, u32[]{:S(2)}, u32[]{:S(2)}) %collective-permute-start.12) | collective-permute-done | bytes 221216 | tf_op jit(solution)/shard_map/ppermute | solution.py:49
  100.5 5.8 %collective-permute-done.13 = f32[2,48,576]{2,1,0:T(8,128)S(1)} collective-permute-done((f32[2,48,576]{2,1,0:T(8,128)S(1)}, f32[2,48,576]{2,1,0:T(8,128)S(1)}, u32[]{:S(2)}, u32[]{:S(2)}) %collective-permute-start.13) | collective-permute-done | bytes 221216 | tf_op jit(solution)/shard_map/ppermute | solution.py:50
  106.3 0.7 pad_maximum_fusion.34
  107.0 2.0 %collective-permute-start.14 = (f32[6,2,576]{2,1,0:T(2,128)}, f32[6,2,576]{2,1,0:T(2,128)S(1)}, u32[]{:S(2)}, u32[]{:S(2)}) collective-permute-start(f32[6,2,576]{2,1,0:T(2,128)} %get-tuple-element.50), channel_id=1, source_target_pairs={{0,1},{2,3},{4,5},{6,7},{8,9},{10,11},{12,13},{14,15},{16,17},{18,... | collective-permute-start | bytes 82952 | tf_op jit(solution)/shard_map/ppermute | solution.py:49
  109.0 1.4 collective-permute-start.15
  110.5 1.4 convolution_multiply_fusion
  113.2 0.8 copy-done.4
  113.9 0.6 fusion.122
  114.6 0.6 fusion.121
  115.2 8.5 %all-reduce.2 = (f32[96,40]{0,1:T(8,128)S(1)}, f32[96,40]{0,1:T(8,128)S(1)}) all-reduce(f32[96,40]{0,1:T(8,128)S(1)} %fusion.121, f32[96,40]{0,1:T(8,128)S(1)} %fusion.122), channel_id=2, replica_groups=mesh['grp'=2,'gx'=8,'gy'=2] {'grp'}, use_global_device_ids=true, to_apply=%region_0.2.clone | all-reduce | flops 7680 | bytes 61440
  124.0 4.5 %all_gather.14 = f32[2,48,40]{1,0,2:T(2,128)S(1)} all-gather(f32[2,48,20]{1,0,2:T(2,128)S(1)} %copy.312), channel_id=1, replica_groups=mesh['grp'=2,'gx'=8,'gy'=2] {'grp'}, dimensions={2}, use_global_device_ids=true | all-gather | bytes 23040 | tf_op jit(solution)/shard_map/all_gather | solution.py:181
  129.2 3.1 %collective-permute-done.20 = f32[1,2,48,20]{2,3,1,0:T(8,128)S(1)} collective-permute-done((f32[1,2,48,20]{2,3,1,0:T(8,128)S(1)}, f32[1,2,48,20]{2,3,1,0:T(8,128)S(1)}, u32[]{:S(2)}, u32[]{:S(2)}) %collective-permute-start.20) | collective-permute-done | bytes 7712 | tf_op jit(solution)/shard_map/ppermute | solution.py:29
  132.5 1.9 %collective-permute-start.21 = (f32[1,48,40]{1,2,0:T(8,128)S(1)}, f32[1,48,40]{1,2,0:T(8,128)S(1)}, u32[]{:S(2)}, u32[]{:S(2)}) collective-permute-start(f32[1,48,40]{1,2,0:T(8,128)S(1)} %get-tuple-element.81), channel_id=1, source_target_pairs={{2,0},{4,2},{6,4},{8,6},{10,8},{12,10},{14,12},{3,1},{5,3},{7,5},{... | collective-permute-start | bytes 23048 | tf_op jit(solution)/shard_map/ppermute | solution.py:50
  134.5 3.9 %collective-permute-start.22 = (f32[1,48,40]{1,2,0:T(8,128)S(1)}, f32[1,48,40]{1,2,0:T(8,128)S(1)}, u32[]{:S(2)}, u32[]{:S(2)}) collective-permute-start(f32[1,48,40]{1,2,0:T(8,128)S(1)} %get-tuple-element.80), channel_id=1, source_target_pairs={{0,2},{2,4},{4,6},{6,8},{8,10},{10,12},{12,14},{1,3},{3,5},{5,7},{... | collective-permute-start | bytes 23048 | tf_op jit(solution)/shard_map/ppermute | solution.py:49
  138.4 2.6 %collective-permute-done.22 = f32[1,48,40]{1,2,0:T(8,128)S(1)} collective-permute-done((f32[1,48,40]{1,2,0:T(8,128)S(1)}, f32[1,48,40]{1,2,0:T(8,128)S(1)}, u32[]{:S(2)}, u32[]{:S(2)}) %collective-permute-start.22) | collective-permute-done | bytes 7712 | tf_op jit(solution)/shard_map/ppermute | solution.py:49
  141.1 1.3 collective-permute-start.23
  142.4 3.0 %collective-permute-start.24 = (f32[4,1,40]{1,2,0:T(8,128)S(1)}, f32[4,1,40]{1,2,0:T(8,128)S(1)}, u32[]{:S(2)}, u32[]{:S(2)}) collective-permute-start(f32[4,1,40]{1,2,0:T(8,128)S(1)} %get-tuple-element.73), channel_id=1, source_target_pairs={{0,1},{2,3},{4,5},{6,7},{8,9},{10,11},{12,13},{14,15},{16,17},{18,... | collective-permute-start | bytes 1928 | tf_op jit(solution)/shard_map/ppermute | solution.py:49
  145.5 0.9 collective-permute-done.24
  147.2 4.5 %all_gather.15 = f32[2,48,40]{1,0,2:T(2,128)S(1)} all-gather(f32[2,48,20]{1,0,2:T(2,128)S(1)} %copy.320), channel_id=1, replica_groups=mesh['grp'=2,'gx'=8,'gy'=2] {'grp'}, dimensions={2}, use_global_device_ids=true | all-gather | bytes 23040 | tf_op jit(solution)/shard_map/all_gather | solution.py:181
  (149 shorter events, 12.9 us)
Async XLA Ops:
  0.6 32.1 %copy-start = (bf16[512,576]{0,1:T(8,128)(2,1)S(1)}, bf16[512,576]{0,1:T(8,128)(2,1)}, u32[]{:S(2)}) copy-start(bf16[512,576]{0,1:T(8,128)(2,1)} %param.22) | copy-start | bytes 1769476
  0.6 0.7 copy-start.29
  0.7 0.8 copy-start.17
  6.0 0.7 copy-start.26
  7.1 0.8 copy-start.18
  12.4 7.8 %copy-start.28 = (s32[2,48]{1,0:T(2,128)S(1)}, s32[2,48]{1,0:T(2,128)}, u32[]{:S(2)}) copy-start(s32[2,48]{1,0:T(2,128)} %param.14) | copy-start | bytes 1156
  12.4 7.8 %copy-start.13 = (f32[2,48,576]{2,1,0:T(8,128)S(1)}, f32[2,48,576]{2,1,0:T(8,128)}, u32[]{:S(2)}) copy-start(f32[2,48,576]{2,1,0:T(8,128)} %param.13) | copy-start | bytes 663556
  13.0 19.5 %copy-start.1 = (bf16[576,512]{1,0:T(8,128)(2,1)S(1)}, bf16[576,512]{1,0:T(8,128)(2,1)}, u32[]{:S(2)}) copy-start(bf16[576,512]{1,0:T(8,128)(2,1)} %param.20) | copy-start | bytes 1769476
  13.4 35.2 %collective-permute-start.4 = (f32[2,48,32]{1,0,2:T(2,128)S(1)}, f32[2,48,32]{1,0,2:T(2,128)}, u32[]{:S(2)}, u32[]{:S(2)}) collective-permute-start(f32[2,48,32]{1,0,2:T(2,128)S(1)} %constant_dynamic-update-slice_fusion), channel_id=1, source_target_pairs={{0,2},{2,4},{4,6},{6,8},{8,10},{10,12},{12,14},{1,3},{3,5},{5,7},{... | collective-permute-start | bytes 36872 | tf_op jit(solution)/shard_map/ppermute | solution.py:49
  16.8 31.8 %collective-permute-start.5 = (f32[2,48,32]{1,0,2:T(2,128)S(1)}, f32[2,48,32]{1,0,2:T(2,128)}, u32[]{:S(2)}, u32[]{:S(2)}) collective-permute-start(f32[2,48,32]{1,0,2:T(2,128)S(1)} %constant_dynamic-update-slice_fusion), channel_id=1, source_target_pairs={{2,0},{4,2},{6,4},{8,6},{10,8},{12,10},{14,12},{3,1},{5,3},{7,5},{... | collective-permute-start | bytes 36872 | tf_op jit(solution)/shard_map/ppermute | solution.py:50
  20.2 0.6 copy-start.19
  20.2 12.3 %copy-start.27 = (f32[40,32]{0,1:T(8,128)S(1)}, f32[40,32]{0,1:T(8,128)}, u32[]{:S(2)}) copy-start(f32[40,32]{0,1:T(8,128)} %param.19) | copy-start | bytes 15364
  20.8 12.0 %copy-start.2 = (bf16[576,512]{1,0:T(8,128)(2,1)S(1)}, bf16[576,512]{1,0:T(8,128)(2,1)}, u32[]{:S(2)}) copy-start(bf16[576,512]{1,0:T(8,128)(2,1)} %param.21) | copy-start | bytes 1769476
  20.8 31.4 %collective-permute-start = (f32[2,48,576]{2,1,0:T(8,128)S(1)}, f32[2,48,576]{2,1,0:T(8,128)S(1)}, u32[]{:S(2)}, u32[]{:S(2)}) collective-permute-start(f32[2,48,576]{2,1,0:T(8,128)S(1)} %get-tuple-element.49), channel_id=1, source_target_pairs={{0,2},{2,4},{4,6},{6,8},{8,10},{10,12},{12,14},{1,3},{3,5},{5,7},{... | collective-permute-start | bytes 663560 | tf_op jit(solution)/shard_map/ppermute | solution.py:49
  24.6 12.0 %collective-permute-start.16 = (f32[1,48,40]{1,2,0:T(8,128)}, f32[1,48,40]{1,2,0:T(8,128)}, u32[]{:S(2)}, u32[]{:S(2)}) collective-permute-start(f32[1,48,40]{1,2,0:T(8,128)} %get-tuple-element.85), channel_id=1, source_target_pairs={{2,0},{4,2},{6,4},{8,6},{10,8},{12,10},{14,12},{3,1},{5,3},{7,5},{... | collective-permute-start | bytes 23048 | tf_op jit(solution)/shard_map/ppermute | solution.py:50
  28.3 8.4 %collective-permute-start.17 = (f32[1,48,40]{1,2,0:T(8,128)}, f32[1,48,40]{1,2,0:T(8,128)}, u32[]{:S(2)}, u32[]{:S(2)}) collective-permute-start(f32[1,48,40]{1,2,0:T(8,128)} %get-tuple-element.84), channel_id=1, source_target_pairs={{0,2},{2,4},{4,6},{6,8},{8,10},{10,12},{12,14},{1,3},{3,5},{5,7},{... | collective-permute-start | bytes 23048 | tf_op jit(solution)/shard_map/ppermute | solution.py:49
  37.5 6.2 %collective-permute-start.18 = (f32[4,1,40]{1,2,0:T(8,128)S(1)}, f32[4,1,40]{1,2,0:T(8,128)S(1)}, u32[]{:S(2)}, u32[]{:S(2)}) collective-permute-start(f32[4,1,40]{1,2,0:T(8,128)S(1)} %get-tuple-element.76), channel_id=1, source_target_pairs={{1,0},{3,2},{5,4},{7,6},{9,8},{11,10},{13,12},{15,14},{17,16},{19,... | collective-permute-start | bytes 1928 | tf_op jit(solution)/shard_map/ppermute | solution.py:50
  38.8 8.9 %collective-permute-start.19 = (f32[4,1,40]{1,2,0:T(8,128)S(1)}, f32[4,1,40]{1,2,0:T(8,128)S(1)}, u32[]{:S(2)}, u32[]{:S(2)}) collective-permute-start(f32[4,1,40]{1,2,0:T(8,128)S(1)} %get-tuple-element.77), channel_id=1, source_target_pairs={{0,1},{2,3},{4,5},{6,7},{8,9},{10,11},{12,13},{14,15},{16,17},{18,... | collective-permute-start | bytes 1928 | tf_op jit(solution)/shard_map/ppermute | solution.py:49
  41.8 0.7 copy-start.30
  43.8 9.1 %collective-permute-start.1 = (f32[2,48,576]{2,1,0:T(8,128)S(1)}, f32[2,48,576]{2,1,0:T(8,128)S(1)}, u32[]{:S(2)}, u32[]{:S(2)}) collective-permute-start(f32[2,48,576]{2,1,0:T(8,128)S(1)} %get-tuple-element.49), channel_id=1, source_target_pairs={{2,0},{4,2},{6,4},{8,6},{10,8},{12,10},{14,12},{3,1},{5,3},{7,5},{... | collective-permute-start | bytes 663560 | tf_op jit(solution)/shard_map/ppermute | solution.py:50
  49.6 8.4 %collective-permute-start.6 = (f32[6,2,32]{1,0,2:T(8,128)S(1)}, f32[6,2,32]{1,0,2:T(8,128)S(1)}, u32[]{:S(2)}, u32[]{:S(2)}) collective-permute-start(f32[6,2,32]{1,0,2:T(8,128)S(1)} %get-tuple-element.68), channel_id=1, source_target_pairs={{0,1},{2,3},{4,5},{6,7},{8,9},{10,11},{12,13},{14,15},{16,17},{18,... | collective-permute-start | bytes 4616 | tf_op jit(solution)/shard_map/ppermute | solution.py:49
  50.9 7.1 %collective-permute-start.7 = (f32[6,2,32]{1,0,2:T(8,128)S(1)}, f32[6,2,32]{1,0,2:T(8,128)S(1)}, u32[]{:S(2)}, u32[]{:S(2)}) collective-permute-start(f32[6,2,32]{1,0,2:T(8,128)S(1)} %get-tuple-element.69), channel_id=1, source_target_pairs={{1,0},{3,2},{5,4},{7,6},{9,8},{11,10},{13,12},{15,14},{17,16},{19,... | collective-permute-start | bytes 4616 | tf_op jit(solution)/shard_map/ppermute | solution.py:50
  52.2 1.4 copy-start.5
  52.9 0.7 copy-start.6
  53.6 5.5 %collective-permute-start.2 = (f32[6,2,576]{2,1,0:T(2,128)}, f32[6,2,576]{2,1,0:T(2,128)}, u32[]{:S(2)}, u32[]{:S(2)}) collective-permute-start(f32[6,2,576]{2,1,0:T(2,128)} %get-tuple-element.54), channel_id=1, source_target_pairs={{0,1},{2,3},{4,5},{6,7},{8,9},{10,11},{12,13},{14,15},{16,17},{18,... | collective-permute-start | bytes 82952 | tf_op jit(solution)/shard_map/ppermute | solution.py:49
  56.6 3.4 %collective-permute-start.3 = (f32[6,2,576]{2,1,0:T(2,128)}, f32[6,2,576]{2,1,0:T(2,128)}, u32[]{:S(2)}, u32[]{:S(2)}) collective-permute-start(f32[6,2,576]{2,1,0:T(2,128)} %get-tuple-element.55), channel_id=1, source_target_pairs={{1,0},{3,2},{5,4},{7,6},{9,8},{11,10},{13,12},{15,14},{17,16},{19,... | collective-permute-start | bytes 82952 | tf_op jit(solution)/shard_map/ppermute | solution.py:50
  60.1 1.2 copy-start.22
  61.3 0.7 copy-start.21
  62.2 0.9 copy-start.11
  62.2 1.1 copy-start.12
  62.4 0.8 copy-start.25
  62.4 0.8 copy-start.24
  62.4 0.8 copy-start.23
  62.4 0.8 copy-start.20
  63.4 11.5 %collective-permute-start.8 = (f32[2,48,576]{2,1,0:T(8,128)S(1)}, f32[2,48,576]{2,1,0:T(8,128)S(1)}, u32[]{:S(2)}, u32[]{:S(2)}) collective-permute-start(f32[2,48,576]{2,1,0:T(8,128)S(1)} %get-tuple-element.46), channel_id=1, source_target_pairs={{0,2},{2,4},{4,6},{6,8},{8,10},{10,12},{12,14},{1,3},{3,5},{5,7},{... | collective-permute-start | bytes 663560 | tf_op jit(solution)/shard_map/ppermute | solution.py:49
  65.4 14.8 %collective-permute-start.9 = (f32[2,48,576]{2,1,0:T(8,128)S(1)}, f32[2,48,576]{2,1,0:T(8,128)S(1)}, u32[]{:S(2)}, u32[]{:S(2)}) collective-permute-start(f32[2,48,576]{2,1,0:T(8,128)S(1)} %get-tuple-element.46), channel_id=1, source_target_pairs={{2,0},{4,2},{6,4},{8,6},{10,8},{12,10},{14,12},{3,1},{5,3},{7,5},{... | collective-permute-start | bytes 663560 | tf_op jit(solution)/shard_map/ppermute | solution.py:50
  80.1 0.7 copy-start.9
  80.8 6.0 %collective-permute-start.10 = (f32[6,2,576]{2,1,0:T(2,128)}, f32[6,2,576]{2,1,0:T(2,128)}, u32[]{:S(2)}, u32[]{:S(2)}) collective-permute-start(f32[6,2,576]{2,1,0:T(2,128)} %get-tuple-element.52), channel_id=1, source_target_pairs={{0,1},{2,3},{4,5},{6,7},{8,9},{10,11},{12,13},{14,15},{16,17},{18,... | collective-permute-start | bytes 82952 | tf_op jit(solution)/shard_map/ppermute | solution.py:49
  83.4 3.4 %collective-permute-start.11 = (f32[6,2,576]{2,1,0:T(2,128)}, f32[6,2,576]{2,1,0:T(2,128)}, u32[]{:S(2)}, u32[]{:S(2)}) collective-permute-start(f32[6,2,576]{2,1,0:T(2,128)} %get-tuple-element.53), channel_id=1, source_target_pairs={{1,0},{3,2},{5,4},{7,6},{9,8},{11,10},{13,12},{15,14},{17,16},{19,... | collective-permute-start | bytes 82952 | tf_op jit(solution)/shard_map/ppermute | solution.py:50
  88.3 0.9 copy-start.10
  89.5 11.0 %collective-permute-start.12 = (f32[2,48,576]{2,1,0:T(8,128)S(1)}, f32[2,48,576]{2,1,0:T(8,128)S(1)}, u32[]{:S(2)}, u32[]{:S(2)}) collective-permute-start(f32[2,48,576]{2,1,0:T(8,128)S(1)} %get-tuple-element.44), channel_id=1, source_target_pairs={{0,2},{2,4},{4,6},{6,8},{8,10},{10,12},{12,14},{1,3},{3,5},{5,7},{... | collective-permute-start | bytes 663560 | tf_op jit(solution)/shard_map/ppermute | solution.py:49
  91.4 14.9 %collective-permute-start.13 = (f32[2,48,576]{2,1,0:T(8,128)S(1)}, f32[2,48,576]{2,1,0:T(8,128)S(1)}, u32[]{:S(2)}, u32[]{:S(2)}) collective-permute-start(f32[2,48,576]{2,1,0:T(8,128)S(1)} %get-tuple-element.44), channel_id=1, source_target_pairs={{2,0},{4,2},{6,4},{8,6},{10,8},{12,10},{14,12},{3,1},{5,3},{7,5},{... | collective-permute-start | bytes 663560 | tf_op jit(solution)/shard_map/ppermute | solution.py:50
  106.3 0.7 copy-start.7
  107.0 4.9 %collective-permute-start.14 = (f32[6,2,576]{2,1,0:T(2,128)}, f32[6,2,576]{2,1,0:T(2,128)S(1)}, u32[]{:S(2)}, u32[]{:S(2)}) collective-permute-start(f32[6,2,576]{2,1,0:T(2,128)} %get-tuple-element.50), channel_id=1, source_target_pairs={{0,1},{2,3},{4,5},{6,7},{8,9},{10,11},{12,13},{14,15},{16,17},{18,... | collective-permute-start | bytes 82952 | tf_op jit(solution)/shard_map/ppermute | solution.py:49
  109.0 3.2 %copy-start.8 = (f32[2,48,576]{2,1,0:T(8,128)S(1)}, f32[2,48,576]{2,1,0:T(8,128)}, u32[]{:S(2)}) copy-start(f32[2,48,576]{2,1,0:T(8,128)} %copy-done.7) | copy-start | bytes 663556
  109.0 3.2 %collective-permute-start.15 = (f32[6,2,576]{2,1,0:T(2,128)S(1)}, f32[6,2,576]{2,1,0:T(2,128)S(1)}, u32[]{:S(2)}, u32[]{:S(2)}) collective-permute-start(f32[6,2,576]{2,1,0:T(2,128)S(1)} %get-tuple-element.51), channel_id=1, source_target_pairs={{1,0},{3,2},{5,4},{7,6},{9,8},{11,10},{13,12},{15,14},{17,16},{19,... | collective-permute-start | bytes 82952 | tf_op jit(solution)/shard_map/ppermute | solution.py:50
  113.0 1.0 copy-start.4
  113.1 1.4 copy-start.3
  114.6 14.4 %copy-start.14 = (f32[40,20]{0,1:T(8,128)S(1)}, f32[40,20]{0,1:T(8,128)}, u32[]{:S(2)}) copy-start(f32[40,20]{0,1:T(8,128)} %param.23) | copy-start | bytes 9604
  123.8 22.7 %copy-start.15 = (f32[2,48,20]{1,0,2:T(2,128)}, f32[2,48,20]{1,0,2:T(2,128)S(1)}, u32[]{:S(2)}) copy-start(f32[2,48,20]{1,0,2:T(2,128)S(1)} %reshape.214) | copy-start | bytes 23044
  124.0 22.5 %copy-start.16 = (f32[2,48,20]{1,0,2:T(2,128)}, f32[2,48,20]{1,0,2:T(2,128)S(1)}, u32[]{:S(2)}) copy-start(f32[2,48,20]{1,0,2:T(2,128)S(1)} %reshape.215) | copy-start | bytes 23044
  128.5 3.8 %collective-permute-start.20 = (f32[1,2,48,20]{2,3,1,0:T(8,128)S(1)}, f32[1,2,48,20]{2,3,1,0:T(8,128)S(1)}, u32[]{:S(2)}, u32[]{:S(2)}) collective-permute-start(f32[1,2,48,20]{2,3,1,0:T(8,128)S(1)} %bitcast.82), channel_id=1, source_target_pairs={{0,16},{16,0},{1,17},{17,1},{2,18},{18,2},{3,19},{19,3},{4,20},{20... | collective-permute-start | bytes 23048 | tf_op jit(solution)/shard_map/ppermute | solution.py:29
  132.5 5.9 %collective-permute-start.21 = (f32[1,48,40]{1,2,0:T(8,128)S(1)}, f32[1,48,40]{1,2,0:T(8,128)S(1)}, u32[]{:S(2)}, u32[]{:S(2)}) collective-permute-start(f32[1,48,40]{1,2,0:T(8,128)S(1)} %get-tuple-element.81), channel_id=1, source_target_pairs={{2,0},{4,2},{6,4},{8,6},{10,8},{12,10},{14,12},{3,1},{5,3},{7,5},{... | collective-permute-start | bytes 23048 | tf_op jit(solution)/shard_map/ppermute | solution.py:50
  134.5 6.6 %collective-permute-start.22 = (f32[1,48,40]{1,2,0:T(8,128)S(1)}, f32[1,48,40]{1,2,0:T(8,128)S(1)}, u32[]{:S(2)}, u32[]{:S(2)}) collective-permute-start(f32[1,48,40]{1,2,0:T(8,128)S(1)} %get-tuple-element.80), channel_id=1, source_target_pairs={{0,2},{2,4},{4,6},{6,8},{8,10},{10,12},{12,14},{1,3},{3,5},{5,7},{... | collective-permute-start | bytes 23048 | tf_op jit(solution)/shard_map/ppermute | solution.py:49
  141.1 4.3 %collective-permute-start.23 = (f32[4,1,40]{1,2,0:T(8,128)S(1)}, f32[4,1,40]{1,2,0:T(8,128)S(1)}, u32[]{:S(2)}, u32[]{:S(2)}) collective-permute-start(f32[4,1,40]{1,2,0:T(8,128)S(1)} %get-tuple-element.72), channel_id=1, source_target_pairs={{1,0},{3,2},{5,4},{7,6},{9,8},{11,10},{13,12},{15,14},{17,16},{19,... | collective-permute-start | bytes 1928 | tf_op jit(solution)/shard_map/ppermute | solution.py:50
  142.4 3.9 %collective-permute-start.24 = (f32[4,1,40]{1,2,0:T(8,128)S(1)}, f32[4,1,40]{1,2,0:T(8,128)S(1)}, u32[]{:S(2)}, u32[]{:S(2)}) collective-permute-start(f32[4,1,40]{1,2,0:T(8,128)S(1)} %get-tuple-element.73), channel_id=1, source_target_pairs={{0,1},{2,3},{4,5},{6,7},{8,9},{10,11},{12,13},{14,15},{16,17},{18,... | collective-permute-start | bytes 1928 | tf_op jit(solution)/shard_map/ppermute | solution.py:49
  146.5 5.9 %collective-permute-start.25 = (f32[1,2,48,20]{2,3,1,0:T(8,128)S(1)}, f32[1,2,48,20]{2,3,1,0:T(8,128)S(1)}, u32[]{:S(2)}, u32[]{:S(2)}) collective-permute-start(f32[1,2,48,20]{2,3,1,0:T(8,128)S(1)} %bitcast.81), channel_id=1, source_target_pairs={{0,16},{16,0},{1,17},{17,1},{2,18},{18,2},{3,19},{19,3},{4,20},{20... | collective-permute-start | bytes 23048 | tf_op jit(solution)/shard_map/ppermute | solution.py:29
